TPU v7x, 256 devices: a whole 4x4x8 slice. The times are simulated.
256 devices in a mesh: rows: 64 (over y, z, core), feat: 4 (over x).
Axes of the slice: x: 4, y: 4, z: 8, core: 2. Of those that a mesh axis runs over, the one named last changes fastest.
Arguments:
- gradients: bfloat16 [32768, 128], P('rows'), may hold values from -6 to 6
- hessians: bfloat16 [32768], P('rows'), may hold values from 0.25 to 2
- bin_words: int32 [128, 32768], P('feat', 'rows'), may hold values from 0 to 4095, as said below
- children: int32 [3, 32768], P(None, 'rows'), may hold values from 0 to 1, as said below
- split_feature: int32 [14], replicated, may hold values from 0 to 255
- split_bin: int32 [14], replicated, may hold values from 0 to 62
Outputs:
- split_gain_one: float32 [128, 256], P('rows', 'feat')
- split_gain_two: float32 [256, 256], P('rows', 'feat')
- split_gain_three: float32 [512, 256], P('rows', 'feat')
- child_scores: float32 [3, 64, 2, 128], P(None, 'rows')
Inputs may be any that keep to these rules, and one draw needn't show every extreme that they name: `children`: of the 512 rows of one device, at most 3 / 4, 1 / 2 and 1 / 4 of 512 lie in one node at depths 1, 2 and 3; every device reaches each of these bounds in some node. `bin_words`: word w of panel p, six bits a feature with the lowest bits first, holds the bins of the panel's features 2 w and 2 w + 1, numbered within the panel of 64 features; slots past the panel's last feature are zero. Every bin is below 64.
All inputs are finite; a program needn't handle non-finite values.
Results may differ from a plain program's by a relative error of at most 0.0003.
Values may be sent and summed in bfloat16 or wider, within the bound.
A program may use at most 64 MiB of HBM per device.

v0:
```python
import jax
import jax.numpy as jnp
from jax import lax
from jax.sharding import PartitionSpec as P

FEATURES = 256
BINS = 64
OUT = 128
LEVELS = 3
penalty = 1.0


def as_sent(array):
    return jax.tree.map(lambda a: a.astype(jnp.bfloat16) if a.dtype == jnp.float32 else a, array)


def swapped(block, axis, stride):
    count = lax.axis_size(axis)
    route = []
    for low in range(count):
        high = low | 1 << stride
        if high != low and high < count:
            route += [(low, high), (high, low)]
    return lax.ppermute(block, axis, route)


def unpack_codes(packed):
    shifts = 6 * jnp.arange(2, dtype=jnp.int32)
    pieces = jnp.bitwise_and(jnp.right_shift(packed[:, None, :], shifts[None, :, None]), 63)
    return pieces.reshape(-1, packed.shape[-1])


def split_terms(cumulative, hess_cum):
    total_sum = cumulative[..., -1:, :]
    hess_total = hess_cum[..., -1:]
    right_sum = total_sum - cumulative
    hess_right = hess_total - hess_cum
    split_score = (
        jnp.sum(cumulative * cumulative, -1) / (hess_cum + penalty)
        + jnp.sum(right_sum * right_sum, -1) / (hess_right + penalty)
        - jnp.sum(total_sum * total_sum, -1) / (hess_total + penalty)
    ) / OUT
    return (split_score, right_sum, hess_right)


def front_index(marked, slot_total):
    running = jnp.cumsum(marked.astype(jnp.int32))
    wanted = jnp.arange(slot_total, dtype=jnp.int32) + 1
    source = jnp.searchsorted(running, wanted, side="left")
    filled = wanted <= running[-1]
    return (jnp.minimum(source, marked.shape[0] - 1), filled)


def pick_rows(values, source, filled):
    taken = jnp.take(values, source, axis=0)
    return jnp.where(filled[:, None], taken, jnp.zeros_like(taken))


def pick_slots(values, source, filled):
    taken = jnp.take(values, source, axis=0)
    return jnp.where(filled, taken, jnp.zeros_like(taken))


def pick_columns(values, source, filled):
    taken = jnp.take(values, source, axis=1)
    return jnp.where(filled[None, :], taken, jnp.zeros_like(taken))


def build_hist(bin_codes, grad_rows, hess_rows, block_rows):
    feat_count = bin_codes.shape[0]
    bin_levels = jnp.arange(BINS, dtype=jnp.int32)

    def add_block(step_index, running):
        start_row = step_index * block_rows
        code_block = lax.dynamic_slice_in_dim(bin_codes, start_row, block_rows, 1)
        grad_block = lax.dynamic_slice_in_dim(grad_rows, start_row, block_rows, 0)
        hess_block = lax.dynamic_slice_in_dim(hess_rows, start_row, block_rows, 0)
        one_hot = (code_block[:, None, :] == bin_levels[None, :, None]).astype(jnp.bfloat16)
        one_hot = one_hot.reshape(feat_count * BINS, block_rows)
        return (
            running[0] + jnp.dot(one_hot, grad_block, preferred_element_type=jnp.float32),
            running[1] + jnp.dot(one_hot, hess_block, preferred_element_type=jnp.float32),
        )

    initial = (
        jnp.zeros((feat_count * BINS, OUT), jnp.float32),
        jnp.zeros((feat_count * BINS,), jnp.float32),
    )
    return lax.fori_loop(0, grad_rows.shape[0] // block_rows, add_block, initial)


def on_device(gradients, hessians, bin_words, children, split_feature, split_bin):
    row_count = lax.axis_size("rows")
    top_bit = row_count.bit_length() - 1
    row_index = lax.axis_index("rows")
    panel_index = lax.axis_index("feat")
    feat_dev = FEATURES // lax.axis_size("feat")
    row_dev = gradients.shape[0]
    slot_count = 2 * row_dev
    block_rows = min(256, slot_count)
    pad_rows = slot_count - row_dev
    grad_rows = jnp.concatenate([gradients, jnp.zeros((pad_rows, OUT), jnp.bfloat16)], 0)
    hess_rows = jnp.concatenate([hessians, jnp.zeros((pad_rows,), jnp.bfloat16)], 0)
    word_rows = jnp.concatenate(
        [bin_words, jnp.zeros((bin_words.shape[0], pad_rows), jnp.int32)], 1
    )
    child_rows = jnp.concatenate([children, jnp.zeros((children.shape[0], pad_rows), jnp.int32)], 1)
    splits_total = split_feature.shape[0]
    collected = jnp.zeros((splits_total, 2, OUT), jnp.float32)
    gain_list = []
    slot_list = []
    for level_index in range(LEVELS):
        cross_bit = top_bit - 1 - level_index
        half_bit = jnp.bitwise_and(jnp.right_shift(row_index, cross_bit), 1)
        living = hess_rows > 0
        staying = living & (child_rows[level_index] == half_bit)
        leaving = living & (child_rows[level_index] != half_bit)
        sent_hess = jnp.where(leaving, hess_rows, jnp.zeros_like(hess_rows))
        got_grad, got_hess, got_words, got_child = (
            swapped(grad_rows, "rows", cross_bit),
            swapped(sent_hess, "rows", cross_bit),
            swapped(as_sent(word_rows), "rows", cross_bit).astype(word_rows.dtype),
            swapped(as_sent(child_rows), "rows", cross_bit).astype(child_rows.dtype),
        )
        accepted = jnp.concatenate([staying, got_hess > 0])
        source, filled = front_index(accepted, slot_count)
        grad_rows = pick_rows(jnp.concatenate([grad_rows, got_grad], 0), source, filled)
        hess_rows = pick_slots(jnp.concatenate([hess_rows, got_hess], 0), source, filled)
        word_rows = pick_columns(jnp.concatenate([word_rows, got_words], 1), source, filled)
        child_rows = pick_columns(jnp.concatenate([child_rows, got_child], 1), source, filled)
        bin_codes = unpack_codes(word_rows)
        hist_grad, hist_hess = build_hist(bin_codes, grad_rows, hess_rows, block_rows)
        group_size = row_count >> level_index + 1
        node_count = 2 ** (level_index + 1)
        node_here = jnp.right_shift(row_index, top_bit - level_index - 1)
        share_grad = hist_grad.reshape(feat_dev, BINS * OUT)
        share_hess = hist_hess.reshape(feat_dev, BINS)
        for step_bit in reversed(range(top_bit - level_index - 1)):
            half_rows = share_grad.shape[0] // 2
            upper_half = jnp.bitwise_and(jnp.right_shift(row_index, step_bit), 1) == 1
            keep_grad = jnp.where(upper_half, share_grad[half_rows:], share_grad[:half_rows])
            give_grad = jnp.where(upper_half, share_grad[:half_rows], share_grad[half_rows:])
            keep_hess = jnp.where(upper_half, share_hess[half_rows:], share_hess[:half_rows])
            give_hess = jnp.where(upper_half, share_hess[:half_rows], share_hess[half_rows:])
            got_partial, got_curv = swapped((give_grad, give_hess), "rows", step_bit)
            share_grad = keep_grad + got_partial
            share_hess = keep_hess + got_curv
        share_count = share_grad.shape[0]
        cumulative = jnp.cumsum(share_grad.reshape(share_count, BINS, OUT), axis=1)
        hess_cum = jnp.cumsum(share_hess, axis=1)
        split_score, right_sum, hess_right = split_terms(cumulative, hess_cum)
        gain_list.append(split_score)
        position = jnp.bitwise_and(row_index, group_size - 1)
        split_slot = node_count - 2 + node_here
        feature_id = split_feature[split_slot]
        bin_id = split_bin[split_slot]
        inner_feature = feature_id % feat_dev
        is_owner = (feature_id // feat_dev == panel_index) & (
            inner_feature // share_count == position
        )
        chosen = (
            (jnp.arange(share_count)[:, None] == inner_feature % share_count)
            & (jnp.arange(BINS)[None, :] == bin_id)
            & is_owner
        )
        left_grad = jnp.sum(jnp.where(chosen[..., None], cumulative, 0.0), axis=(0, 1))
        left_hess = jnp.sum(jnp.where(chosen, hess_cum, 0.0))
        right_grad = jnp.sum(jnp.where(chosen[..., None], right_sum, 0.0), axis=(0, 1))
        right_hess = jnp.sum(jnp.where(chosen, hess_right, 0.0))
        child_pair = jnp.stack(
            [
                -left_grad / jnp.sqrt(left_hess + penalty),
                -right_grad / jnp.sqrt(right_hess + penalty),
            ],
            0,
        )
        slot_match = jnp.arange(splits_total) == split_slot
        collected = collected + jnp.where(slot_match[:, None, None], child_pair[None], 0.0)
        slot_list.append(split_slot)
    totals = lax.psum(collected, ("rows", "feat"))
    child_scores = jnp.stack([totals[slot_index] for slot_index in slot_list], 0)[:, None]
    return (gain_list[0], gain_list[1], gain_list[2], child_scores)


def solution(mesh):
    placed = (P("rows", None), P("rows"), P("feat", "rows"), P(None, "rows"), P(), P())
    return jax.shard_map(
        on_device,
        mesh=mesh,
        in_specs=placed,
        out_specs=(
            P("rows", "feat"),
            P("rows", "feat"),
            P("rows", "feat"),
            P(None, "rows", None, None),
        ),
        check_vma=False,
    )
```

profile of v0, /device:TPU:1, one launch (start us, length us, event | category | flops | bytes accessed | tf_op | source)
XLA Modules:
  0.0 707.1 jit_solution(15301522432196689266)
XLA Ops:
  22.0 74.8 %while.98 = (s32[]{:T(128)}, u32[1024]{0:T(1024)S(1)}, u32[1024]{0:T(1024)S(1)}, s32[2048]{0:T(1024)S(1)}, s32[]{:T(128)}, /*index=5*/s32[]{:T(128)}, s32[]{}) while((s32[]{:T(128)}, u32[1024]{0:T(1024)S(1)}, u32[1024]{0:T(1024)S(1)}, s32[2048]{0:T(1024)S(1)}, s32[]{:T(128)}, /*index=5*/s32[]{:T(128)}, s32[]{}) %tuple.223), condition=%wide.region_3.4_spmd.clone, body=%wide.region_2.3_spmd.clone.sunk | while | flops 20484 | bytes 63589 | solution.py:49
  22.0 6.2 gather_fusion
  28.3 6.2 gather_fusion
  34.5 6.2 gather_fusion
  40.7 6.2 gather_fusion
  97.5 6.8 gather_fusion.5
  112.2 74.8 %while.100 = (s32[]{:T(128)}, u32[1024]{0:T(1024)S(1)}, u32[1024]{0:T(1024)S(1)}, s32[2048]{0:T(1024)S(1)}, s32[]{:T(128)}, /*index=5*/s32[]{:T(128)}, s32[]{}) while((s32[]{:T(128)}, u32[1024]{0:T(1024)S(1)}, u32[1024]{0:T(1024)S(1)}, s32[2048]{0:T(1024)S(1)}, s32[]{:T(128)}, /*index=5*/s32[]{:T(128)}, s32[]{}) %tuple.226), condition=%wide.region_14.19_spmd.clone, body=%wide.region_13.18_spmd.clone.sunk | while | flops 20484 | bytes 63589 | solution.py:49
  188.3 6.8 gather_fusion.9
  199.6 7.0 collective-permute-start.26
  210.8 74.8 %while.102 = (s32[]{:T(128)}, u32[1024]{0:T(1024)S(1)}, u32[1024]{0:T(1024)S(1)}, s32[2048]{0:T(1024)S(1)}, s32[]{:T(128)}, /*index=5*/s32[]{:T(128)}, s32[]{}) while((s32[]{:T(128)}, u32[1024]{0:T(1024)S(1)}, u32[1024]{0:T(1024)S(1)}, s32[2048]{0:T(1024)S(1)}, s32[]{:T(128)}, /*index=5*/s32[]{:T(128)}, s32[]{}) %tuple.229), condition=%wide.region_25.30_spmd.clone, body=%wide.region_24.29_spmd.clone.sunk | while | flops 20484 | bytes 63589 | solution.py:49
  286.2 6.8 gather_fusion.13
  325.9 10.0 %collective-permute-done.27 = s32[32,1024]{0,1:T(8,128)} collective-permute-done((s32[32,1024]{0,1:T(8,128)S(1)}, s32[32,1024]{0,1:T(8,128)}, u32[]{:S(2)}, u32[]{:S(2)}) %collective-permute-start.27) | collective-permute-done | bytes 131104 | tf_op jit(solution)/shard_map/ppermute | solution.py:24
  347.7 14.4 %while.99 = (s32[]{:T(128)}, f32[4096,128]{1,0:T(8,128)S(1)}, f32[4096]{0:T(1024)S(1)}, s32[64,1024]{1,0:T(8,128)}, bf16[1024,128]{1,0:T(8,128)(2,1)S(1)}, /*ind...) while((s32[]{:T(128)}, f32[4096,128]{1,0:T(8,128)S(1)}, ...), condition=%wide.region_5.9_spmd.clone, body=%wide.region_4.8_spmd.clone.sunk | while | flops 272637952 | bytes 7735978 | solution.py:89
  371.3 8.6 %collective-permute-start.10 = (f32[8,64]{1,0:T(8,128)S(1)}, f32[8,64]{1,0:T(8,128)S(1)}, u32[]{:S(2)}, u32[]{:S(2)}) collective-permute-start(f32[8,64]{1,0:T(8,128)S(1)} %slice_select_fusion.26), channel_id=1, source_target_pairs={{0,16},{16,0},{4,20},{20,4},{8,24},{24,8},{12,28},{28,12},{32,48},... | collective-permute-start | bytes 6152 | tf_op jit(solution)/shard_map/ppermute | solution.py:24
  395.3 22.7 %while.101 = (s32[]{:T(128)}, f32[4096,128]{1,0:T(8,128)}, f32[4096]{0:T(1024)S(1)}, s32[64,1024]{1,0:T(8,128)}, bf16[1024,128]{1,0:T(8,128)(2,1)S(1)}, /*index=...) while((s32[]{:T(128)}, f32[4096,128]{1,0:T(8,128)}, ...), condition=%wide.region_16.21_spmd.clone, body=%wide.region_15.20_spmd.clone.sunk | while | flops 272637952 | bytes 7735978 | solution.py:89
  420.2 6.4 collective-permute-start.12
  448.5 17.1 %while.103 = (s32[]{:T(128)}, f32[4096,128]{1,0:T(8,128)S(1)}, f32[4096]{0:T(1024)S(1)}, s32[64,1024]{1,0:T(8,128)}, bf16[1024,128]{1,0:T(8,128)(2,1)S(1)}, /*in...) while((s32[]{:T(128)}, f32[4096,128]{1,0:T(8,128)S(1)}, ...), condition=%wide.region_27.32_spmd.clone, body=%wide.region_26.31_spmd.clone.sunk | while | flops 272637952 | bytes 7735978 | solution.py:89
  465.8 7.1 %collective-permute-start.24 = (f32[4,64]{1,0:T(4,128)S(1)}, f32[4,64]{1,0:T(4,128)S(1)}, u32[]{:S(2)}, u32[]{:S(2)}) collective-permute-start(f32[4,64]{1,0:T(4,128)S(1)} %slice_select_fusion.27), channel_id=1, source_target_pairs={{0,4},{4,0},{8,12},{12,8},{16,20},{20,16},{24,28},{28,24},{32,36},... | collective-permute-start | bytes 3080 | tf_op jit(solution)/shard_map/ppermute | solution.py:24
  472.9 18.8 %collective-permute-done.32 = f32[32,64]{1,0:T(8,128)S(1)} collective-permute-done((f32[32,64]{1,0:T(8,128)S(1)}, f32[32,64]{1,0:T(8,128)S(1)}, u32[]{:S(2)}, u32[]{:S(2)}) %collective-permute-start.32) | collective-permute-done | bytes 8224 | tf_op jit(solution)/shard_map/ppermute | solution.py:24
  508.4 73.3 %collective-permute-done.29 = f32[32,8192]{1,0:T(8,128)} collective-permute-done((f32[32,8192]{1,0:T(8,128)}, f32[32,8192]{1,0:T(8,128)}, u32[]{:S(2)}, u32[]{:S(2)}) %collective-permute-start.29) | collective-permute-done | bytes 1048608 | tf_op jit(solution)/shard_map/ppermute | solution.py:24
  585.3 7.6 %collective-permute-done.18 = f32[16,8192]{1,0:T(8,128)S(1)} collective-permute-done((f32[16,8192]{1,0:T(8,128)S(1)}, f32[16,8192]{1,0:T(8,128)S(1)}, u32[]{:S(2)}, u32[]{:S(2)}) %collective-permute-start.18) | collective-permute-done | bytes 524320 | tf_op jit(solution)/shard_map/ppermute | solution.py:24
  592.9 11.2 %collective-permute-done.5 = f32[8,8192]{1,0:T(8,128)S(1)} collective-permute-done((f32[8,8192]{1,0:T(8,128)S(1)}, f32[8,8192]{1,0:T(8,128)S(1)}, u32[]{:S(2)}, u32[]{:S(2)}) %collective-permute-start.5) | collective-permute-done | bytes 262176 | tf_op jit(solution)/shard_map/ppermute | solution.py:24
  606.1 6.3 collective-permute-done.6
  629.2 76.1 %psum.7 = f32[14,2,128]{2,1,0:T(2,128)S(1)} all-reduce(f32[14,2,128]{2,1,0:T(2,128)S(1)} %select_add_fusion.9), channel_id=1, replica_groups=mesh['rows'=64,'feat'=4] {'rows','feat'}, use_global_device_ids=true, to_apply=%region_45.50 | all-reduce | flops 3584 | bytes 28672 | tf_op jit(solution)/shard_map/psum | solution.py:180
  (596 shorter events, 414.0 us)
Async XLA Ops:
  2.1 18.7 %collective-permute-start = (bf16[1024]{0:T(1024)(128)(2,1)S(1)}, bf16[1024]{0:T(1024)(128)(2,1)S(1)}, u32[]{:S(2)}, u32[]{:S(2)}) collective-permute-start(bf16[1024]{0:T(1024)(128)(2,1)S(1)} %and_select_fusion.2), channel_id=1, source_target_pairs={{0,128},{128,0},{4,132},{132,4},{8,136},{136,8},{12,140},{140,12},... | collective-permute-start | bytes 6152 | tf_op jit(solution)/shard_map/ppermute | solution.py:24
  6.6 97.8 %collective-permute-start.13 = (s32[3,1024]{1,0:T(4,128)S(1)}, s32[3,1024]{1,0:T(4,128)S(1)}, u32[]{:S(2)}, u32[]{:S(2)}) collective-permute-start(s32[3,1024]{1,0:T(4,128)S(1)} %concatenate.74), channel_id=1, source_target_pairs={{0,128},{128,0},{4,132},{132,4},{8,136},{136,8},{12,140},{140,12},... | collective-permute-start | bytes 36872 | tf_op jit(solution)/shard_map/ppermute | solution.py:24
  7.4 285.6 %collective-permute-start.1 = (s32[32,1024]{1,0:T(8,128)S(1)}, s32[32,1024]{1,0:T(8,128)S(1)}, u32[]{:S(2)}, u32[]{:S(2)}) collective-permute-start(s32[32,1024]{1,0:T(8,128)S(1)} %concatenate.78), channel_id=1, source_target_pairs={{0,128},{128,0},{4,132},{132,4},{8,136},{136,8},{12,140},{140,12},... | collective-permute-start | bytes 393224 | tf_op jit(solution)/shard_map/ppermute | solution.py:24
  12.1 306.9 %collective-permute-start.2 = (bf16[1024,128]{1,0:T(8,128)(2,1)}, bf16[1024,128]{1,0:T(8,128)(2,1)}, u32[]{:S(2)}, u32[]{:S(2)}) collective-permute-start(bf16[1024,128]{1,0:T(8,128)(2,1)} %concatenate.80), channel_id=1, source_target_pairs={{0,128},{128,0},{4,132},{132,4},{8,136},{136,8},{12,140},{140,12},... | collective-permute-start | bytes 786440 | tf_op jit(solution)/shard_map/ppermute | solution.py:24
  111.1 84.0 %collective-permute-start.25 = (s32[3,1024]{0,1:T(8,128)S(1)}, s32[3,1024]{0,1:T(8,128)S(1)}, u32[]{:S(2)}, u32[]{:S(2)}) collective-permute-start(s32[3,1024]{0,1:T(8,128)S(1)} %bitcast_select_fusion.2), channel_id=1, source_target_pairs={{0,64},{64,0},{4,68},{68,4},{8,72},{72,8},{12,76},{76,12},{16,80},... | collective-permute-start | bytes 36872 | tf_op jit(solution)/shard_map/ppermute | solution.py:24
  199.6 10.6 %collective-permute-start.26 = (bf16[1024]{0:T(1024)(128)(2,1)S(1)}, bf16[1024]{0:T(1024)(128)(2,1)S(1)}, u32[]{:S(2)}, u32[]{:S(2)}) collective-permute-start(bf16[1024]{0:T(1024)(128)(2,1)S(1)} %and_select_fusion), channel_id=1, source_target_pairs={{0,32},{32,0},{4,36},{36,4},{8,40},{40,8},{12,44},{44,12},{16,48},... | collective-permute-start | bytes 6152 | tf_op jit(solution)/shard_map/ppermute | solution.py:24
  298.8 10.4 %collective-permute-start.15 = (s32[32,1024]{0,1:T(8,128)S(1)}, s32[32,1024]{0,1:T(8,128)}, u32[]{:S(2)}, u32[]{:S(2)}) collective-permute-start(s32[32,1024]{0,1:T(8,128)S(1)} %bitcast_select_fusion.3), channel_id=1, source_target_pairs={{0,64},{64,0},{4,68},{68,4},{8,72},{72,8},{12,76},{76,12},{16,80},... | collective-permute-start | bytes 393224 | tf_op jit(solution)/shard_map/ppermute | solution.py:24
  315.7 20.2 %collective-permute-start.27 = (s32[32,1024]{0,1:T(8,128)S(1)}, s32[32,1024]{0,1:T(8,128)}, u32[]{:S(2)}, u32[]{:S(2)}) collective-permute-start(s32[32,1024]{0,1:T(8,128)S(1)} %bitcast_select_fusion.1), channel_id=1, source_target_pairs={{0,32},{32,0},{4,36},{36,4},{8,40},{40,8},{12,44},{44,12},{16,48},... | collective-permute-start | bytes 393224 | tf_op jit(solution)/shard_map/ppermute | solution.py:24
  371.3 9.9 %collective-permute-start.10 = (f32[8,64]{1,0:T(8,128)S(1)}, f32[8,64]{1,0:T(8,128)S(1)}, u32[]{:S(2)}, u32[]{:S(2)}) collective-permute-start(f32[8,64]{1,0:T(8,128)S(1)} %slice_select_fusion.26), channel_id=1, source_target_pairs={{0,16},{16,0},{4,20},{20,4},{8,24},{24,8},{12,28},{28,12},{32,48},... | collective-permute-start | bytes 6152 | tf_op jit(solution)/shard_map/ppermute | solution.py:24
  379.9 10.8 %collective-permute-start.16 = (bf16[1024,128]{1,0:T(8,128)(2,1)S(1)}, bf16[1024,128]{1,0:T(8,128)(2,1)}, u32[]{:S(2)}, u32[]{:S(2)}) collective-permute-start(bf16[1024,128]{1,0:T(8,128)(2,1)S(1)} %get-tuple-element.1187), channel_id=1, source_target_pairs={{0,64},{64,0},{4,68},{68,4},{8,72},{72,8},{12,76},{76,12},{16,80},... | collective-permute-start | bytes 786440 | tf_op jit(solution)/shard_map/ppermute | solution.py:24
  381.2 9.5 %collective-permute-start.11 = (f32[4,64]{1,0:T(4,128)S(1)}, f32[4,64]{1,0:T(4,128)S(1)}, u32[]{:S(2)}, u32[]{:S(2)}) collective-permute-start(f32[4,64]{1,0:T(4,128)S(1)} %slice_select_fusion.28), channel_id=1, source_target_pairs={{0,8},{8,0},{4,12},{12,4},{16,24},{24,16},{20,28},{28,20},{32,40},... | collective-permute-start | bytes 3080 | tf_op jit(solution)/shard_map/ppermute | solution.py:24
  388.2 112.1 %collective-permute-start.3 = (f32[32,8192]{1,0:T(8,128)}, f32[32,8192]{1,0:T(8,128)}, u32[]{:S(2)}, u32[]{:S(2)}) collective-permute-start(f32[32,8192]{1,0:T(8,128)} %select_n.551), channel_id=1, source_target_pairs={{0,64},{64,0},{4,68},{68,4},{8,72},{72,8},{12,76},{76,12},{16,80},... | collective-permute-start | bytes 3145736 | tf_op jit(solution)/shard_map/ppermute | solution.py:24
  418.1 8.6 %collective-permute-start.21 = (f32[32,64]{1,0:T(8,128)S(1)}, f32[32,64]{1,0:T(8,128)S(1)}, u32[]{:S(2)}, u32[]{:S(2)}) collective-permute-start(f32[32,64]{1,0:T(8,128)S(1)} %select_n.603), channel_id=1, source_target_pairs={{0,32},{32,0},{4,36},{36,4},{8,40},{40,8},{12,44},{44,12},{16,48},... | collective-permute-start | bytes 24584 | tf_op jit(solution)/shard_map/ppermute | solution.py:24
  427.7 16.2 %collective-permute-start.28 = (bf16[1024,128]{1,0:T(8,128)(2,1)S(1)}, bf16[1024,128]{1,0:T(8,128)(2,1)}, u32[]{:S(2)}, u32[]{:S(2)}) collective-permute-start(bf16[1024,128]{1,0:T(8,128)(2,1)S(1)} %get-tuple-element.1189), channel_id=1, source_target_pairs={{0,32},{32,0},{4,36},{36,4},{8,40},{40,8},{12,44},{44,12},{16,48},... | collective-permute-start | bytes 786440 | tf_op jit(solution)/shard_map/ppermute | solution.py:24
  431.2 12.7 %collective-permute-start.23 = (f32[8,64]{1,0:T(8,128)S(1)}, f32[8,64]{1,0:T(8,128)S(1)}, u32[]{:S(2)}, u32[]{:S(2)}) collective-permute-start(f32[8,64]{1,0:T(8,128)S(1)} %slice_select_fusion.25), channel_id=1, source_target_pairs={{0,8},{8,0},{4,12},{12,4},{16,24},{24,16},{20,28},{28,20},{32,40},... | collective-permute-start | bytes 6152 | tf_op jit(solution)/shard_map/ppermute | solution.py:24
  437.7 67.3 %collective-permute-start.17 = (f32[32,8192]{1,0:T(8,128)}, f32[32,8192]{1,0:T(8,128)}, u32[]{:S(2)}, u32[]{:S(2)}) collective-permute-start(f32[32,8192]{1,0:T(8,128)} %select_n.589), channel_id=1, source_target_pairs={{0,32},{32,0},{4,36},{36,4},{8,40},{40,8},{12,44},{44,12},{16,48},... | collective-permute-start | bytes 3145736 | tf_op jit(solution)/shard_map/ppermute | solution.py:24
  465.7 26.0 %collective-permute-start.32 = (f32[32,64]{1,0:T(8,128)S(1)}, f32[32,64]{1,0:T(8,128)S(1)}, u32[]{:S(2)}, u32[]{:S(2)}) collective-permute-start(f32[32,64]{1,0:T(8,128)S(1)} %select_n.632), channel_id=1, source_target_pairs={{0,16},{16,0},{4,20},{20,4},{8,24},{24,8},{12,28},{28,12},{32,48},... | collective-permute-start | bytes 24584 | tf_op jit(solution)/shard_map/ppermute | solution.py:24
  465.8 26.0 %collective-permute-start.24 = (f32[4,64]{1,0:T(4,128)S(1)}, f32[4,64]{1,0:T(4,128)S(1)}, u32[]{:S(2)}, u32[]{:S(2)}) collective-permute-start(f32[4,64]{1,0:T(4,128)S(1)} %slice_select_fusion.27), channel_id=1, source_target_pairs={{0,4},{4,0},{8,12},{12,8},{16,20},{20,16},{24,28},{28,24},{32,36},... | collective-permute-start | bytes 3080 | tf_op jit(solution)/shard_map/ppermute | solution.py:24
  499.5 82.2 %collective-permute-start.29 = (f32[32,8192]{1,0:T(8,128)}, f32[32,8192]{1,0:T(8,128)}, u32[]{:S(2)}, u32[]{:S(2)}) collective-permute-start(f32[32,8192]{1,0:T(8,128)} %select_n.621), channel_id=1, source_target_pairs={{0,16},{16,0},{4,20},{20,4},{8,24},{24,8},{12,28},{28,12},{32,48},... | collective-permute-start | bytes 3145736 | tf_op jit(solution)/shard_map/ppermute | solution.py:24
  501.8 81.4 %collective-permute-start.4 = (f32[16,8192]{1,0:T(8,128)S(1)}, f32[16,8192]{1,0:T(8,128)S(1)}, u32[]{:S(2)}, u32[]{:S(2)}) collective-permute-start(f32[16,8192]{1,0:T(8,128)S(1)} %slice_select_fusion.9), channel_id=1, source_target_pairs={{0,32},{32,0},{4,36},{36,4},{8,40},{40,8},{12,44},{44,12},{16,48},... | collective-permute-start | bytes 1572872 | tf_op jit(solution)/shard_map/ppermute | solution.py:24
  506.4 86.4 %collective-permute-start.18 = (f32[16,8192]{1,0:T(8,128)S(1)}, f32[16,8192]{1,0:T(8,128)S(1)}, u32[]{:S(2)}, u32[]{:S(2)}) collective-permute-start(f32[16,8192]{1,0:T(8,128)S(1)} %slice_select_fusion.8), channel_id=1, source_target_pairs={{0,16},{16,0},{4,20},{20,4},{8,24},{24,8},{12,28},{28,12},{32,48},... | collective-permute-start | bytes 1572872 | tf_op jit(solution)/shard_map/ppermute | solution.py:24
  583.0 35.7 %collective-permute-start.30 = (f32[16,8192]{1,0:T(8,128)S(1)}, f32[16,8192]{1,0:T(8,128)S(1)}, u32[]{:S(2)}, u32[]{:S(2)}) collective-permute-start(f32[16,8192]{1,0:T(8,128)S(1)} %slice_select_fusion.7), channel_id=1, source_target_pairs={{0,8},{8,0},{4,12},{12,4},{16,24},{24,16},{20,28},{28,20},{32,40},... | collective-permute-start | bytes 1572872 | tf_op jit(solution)/shard_map/ppermute | solution.py:24
  583.3 20.8 %collective-permute-start.5 = (f32[8,8192]{1,0:T(8,128)S(1)}, f32[8,8192]{1,0:T(8,128)S(1)}, u32[]{:S(2)}, u32[]{:S(2)}) collective-permute-start(f32[8,8192]{1,0:T(8,128)S(1)} %slice_select_fusion.12), channel_id=1, source_target_pairs={{0,16},{16,0},{4,20},{20,4},{8,24},{24,8},{12,28},{28,12},{32,48},... | collective-permute-start | bytes 786440 | tf_op jit(solution)/shard_map/ppermute | solution.py:24
  604.6 13.4 %collective-permute-start.19 = (f32[8,8192]{1,0:T(8,128)S(1)}, f32[8,8192]{1,0:T(8,128)S(1)}, u32[]{:S(2)}, u32[]{:S(2)}) collective-permute-start(f32[8,8192]{1,0:T(8,128)S(1)} %slice_select_fusion.11), channel_id=1, source_target_pairs={{0,8},{8,0},{4,12},{12,4},{16,24},{24,16},{20,28},{28,20},{32,40},... | collective-permute-start | bytes 786440 | tf_op jit(solution)/shard_map/ppermute | solution.py:24
  (32 other events, 303.9 us)
where the time goes:
time: 718 us; the launch traced here: 707 us
  local copies, waits for them, and re-layouts  310 us (43%)
  waiting for transfers between devices  148 us (21%)
  blocking collectives  76.1 us (11%)
  starting transfers between devices  69.2 us (10%)
  other arithmetic  58 us (8%)
  matrix products  30.3 us (4%)
  between operations  13.7 us (2%)
    gather x36, local copies, waits for them, and re-layouts, front_index(): source = jnp.searchsorted(running, wanted, side='left')  222 us
    ppermute x35, waiting for transfers between devices, swapped(): return lax.ppermute(block, axis, route)  148 us
    psum x1, blocking collectives, on_device(): totals = lax.psum(collected, ('rows', 'feat'))  76.1 us
    ppermute x35, starting transfers between devices, swapped(): return lax.ppermute(block, axis, route)  69.2 us
    dot_general x12, matrix products, add_block(): jnp.dot(one_hot, grad_block, preferred_element_type=jnp.float32)  22.6 us
    gather x3, local copies, waits for them, and re-layouts, pick_slots(): taken = jnp.take(values, source, axis=0)  20.4 us
    gather x5, local copies, waits for them, and re-layouts, pick_columns(): taken = jnp.take(values, source, axis=1)  19 us
  transfers between devices with their start and end apart: 35, of which 14 were waited for; matrix products, arithmetic and copies ran while one was open for 52% of the time, Pallas kernels for 0%

commit v1 on v0

--- a/solution.py
+++ b/solution.py
@@ -177,7 +177,7 @@
         slot_match = jnp.arange(splits_total) == split_slot
         collected = collected + jnp.where(slot_match[:, None, None], child_pair[None], 0.0)
         slot_list.append(split_slot)
-    totals = lax.psum(collected, ("rows", "feat"))
+    totals = lax.psum(lax.psum(collected, "rows"), "feat")
     child_scores = jnp.stack([totals[slot_index] for slot_index in slot_list], 0)[:, None]
     return (gain_list[0], gain_list[1], gain_list[2], child_scores)
 

time: 718 us -> 905 us (1.26)
  blocking collectives: 76.1 us -> 258 us
    psum x1 -> x2, blocking collectives: 76.1 us -> 258 us  [on_device(): totals = lax.psum(lax.psum(collected, 'rows'), 'feat')]
  transfers between devices with their start and end apart: 35 -> 35, of which waited for: 14 -> 14; matrix products, arithmetic and copies ran while one was open for 52% -> 41% of each run, Pallas kernels for 0% -> 0%
where the time goes in v1:
time: 905 us; the launch traced here: 889 us
  local copies, waits for them, and re-layouts  310 us (34%)
  blocking collectives  258 us (29%)
  waiting for transfers between devices  148 us (16%)
  starting transfers between devices  69.2 us (8%)
  other arithmetic  58 us (6%)
  matrix products  30.3 us (3%)
  between operations  13.7 us (2%)
    psum x2, blocking collectives, on_device(): totals = lax.psum(lax.psum(collected, 'rows'), 'feat')  258 us
    gather x36, local copies, waits for them, and re-layouts, front_index(): source = jnp.searchsorted(running, wanted, side='left')  222 us
    ppermute x35, waiting for transfers between devices, swapped(): return lax.ppermute(block, axis, route)  148 us
    ppermute x35, starting transfers between devices, swapped(): return lax.ppermute(block, axis, route)  69.2 us
    dot_general x12, matrix products, add_block(): jnp.dot(one_hot, grad_block, preferred_element_type=jnp.float32)  22.6 us
    gather x3, local copies, waits for them, and re-layouts, pick_slots(): taken = jnp.take(values, source, axis=0)  20.4 us
    gather x5, local copies, waits for them, and re-layouts, pick_columns(): taken = jnp.take(values, source, axis=1)  19 us
  transfers between devices with their start and end apart: 35, of which 14 were waited for; matrix products, arithmetic and copies ran while one was open for 41% of the time, Pallas kernels for 0%

profile of v1, /device:TPU:1, one launch (start us, length us, event | category | flops | bytes accessed | tf_op | source)
XLA Modules:
  0.0 888.7 jit_solution(5603217316353267148)
XLA Ops:
  22.0 74.8 %while.98 = (s32[]{:T(128)}, u32[1024]{0:T(1024)S(1)}, u32[1024]{0:T(1024)S(1)}, s32[2048]{0:T(1024)S(1)}, s32[]{:T(128)}, /*index=5*/s32[]{:T(128)}, s32[]{}) while((s32[]{:T(128)}, u32[1024]{0:T(1024)S(1)}, u32[1024]{0:T(1024)S(1)}, s32[2048]{0:T(1024)S(1)}, s32[]{:T(128)}, /*index=5*/s32[]{:T(128)}, s32[]{}) %tuple.223), condition=%wide.region_3.4_spmd.clone, body=%wide.region_2.3_spmd.clone.sunk | while | flops 20484 | bytes 63589 | solution.py:49
  22.0 6.2 gather_fusion
  28.3 6.2 gather_fusion
  34.5 6.2 gather_fusion
  97.5 6.8 gather_fusion.5
  112.2 74.8 %while.100 = (s32[]{:T(128)}, u32[1024]{0:T(1024)S(1)}, u32[1024]{0:T(1024)S(1)}, s32[2048]{0:T(1024)S(1)}, s32[]{:T(128)}, /*index=5*/s32[]{:T(128)}, s32[]{}) while((s32[]{:T(128)}, u32[1024]{0:T(1024)S(1)}, u32[1024]{0:T(1024)S(1)}, s32[2048]{0:T(1024)S(1)}, s32[]{:T(128)}, /*index=5*/s32[]{:T(128)}, s32[]{}) %tuple.226), condition=%wide.region_14.19_spmd.clone, body=%wide.region_13.18_spmd.clone.sunk | while | flops 20484 | bytes 63589 | solution.py:49
  188.3 6.8 gather_fusion.9
  199.6 7.0 collective-permute-start.26
  210.8 74.8 %while.102 = (s32[]{:T(128)}, u32[1024]{0:T(1024)S(1)}, u32[1024]{0:T(1024)S(1)}, s32[2048]{0:T(1024)S(1)}, s32[]{:T(128)}, /*index=5*/s32[]{:T(128)}, s32[]{}) while((s32[]{:T(128)}, u32[1024]{0:T(1024)S(1)}, u32[1024]{0:T(1024)S(1)}, s32[2048]{0:T(1024)S(1)}, s32[]{:T(128)}, /*index=5*/s32[]{:T(128)}, s32[]{}) %tuple.229), condition=%wide.region_25.30_spmd.clone, body=%wide.region_24.29_spmd.clone.sunk | while | flops 20484 | bytes 63589 | solution.py:49
  286.2 6.8 gather_fusion.13
  325.9 10.0 %collective-permute-done.27 = s32[32,1024]{0,1:T(8,128)} collective-permute-done((s32[32,1024]{0,1:T(8,128)S(1)}, s32[32,1024]{0,1:T(8,128)}, u32[]{:S(2)}, u32[]{:S(2)}) %collective-permute-start.27) | collective-permute-done | bytes 131104 | tf_op jit(solution)/shard_map/ppermute | solution.py:24
  347.7 14.4 %while.99 = (s32[]{:T(128)}, f32[4096,128]{1,0:T(8,128)S(1)}, f32[4096]{0:T(1024)S(1)}, s32[64,1024]{1,0:T(8,128)}, bf16[1024,128]{1,0:T(8,128)(2,1)S(1)}, /*ind...) while((s32[]{:T(128)}, f32[4096,128]{1,0:T(8,128)S(1)}, ...), condition=%wide.region_5.9_spmd.clone, body=%wide.region_4.8_spmd.clone.sunk | while | flops 272637952 | bytes 7735978 | solution.py:89
  371.3 8.6 collective-permute-start.10
  395.3 22.7 %while.101 = (s32[]{:T(128)}, f32[4096,128]{1,0:T(8,128)}, f32[4096]{0:T(1024)S(1)}, s32[64,1024]{1,0:T(8,128)}, bf16[1024,128]{1,0:T(8,128)(2,1)S(1)}, /*index=...) while((s32[]{:T(128)}, f32[4096,128]{1,0:T(8,128)}, ...), condition=%wide.region_16.21_spmd.clone, body=%wide.region_15.20_spmd.clone.sunk | while | flops 272637952 | bytes 7735978 | solution.py:89
  420.2 6.4 collective-permute-start.12
  448.5 17.1 %while.103 = (s32[]{:T(128)}, f32[4096,128]{1,0:T(8,128)S(1)}, f32[4096]{0:T(1024)S(1)}, s32[64,1024]{1,0:T(8,128)}, bf16[1024,128]{1,0:T(8,128)(2,1)S(1)}, /*in...) while((s32[]{:T(128)}, f32[4096,128]{1,0:T(8,128)S(1)}, ...), condition=%wide.region_27.32_spmd.clone, body=%wide.region_26.31_spmd.clone.sunk | while | flops 272637952 | bytes 7735978 | solution.py:89
  465.8 7.1 collective-permute-start.24
  472.9 18.8 %collective-permute-done.32 = f32[32,64]{1,0:T(8,128)S(1)} collective-permute-done((f32[32,64]{1,0:T(8,128)S(1)}, f32[32,64]{1,0:T(8,128)S(1)}, u32[]{:S(2)}, u32[]{:S(2)}) %collective-permute-start.32) | collective-permute-done | bytes 8224 | tf_op jit(solution)/shard_map/ppermute | solution.py:24
  508.4 73.3 %collective-permute-done.29 = f32[32,8192]{1,0:T(8,128)} collective-permute-done((f32[32,8192]{1,0:T(8,128)}, f32[32,8192]{1,0:T(8,128)}, u32[]{:S(2)}, u32[]{:S(2)}) %collective-permute-start.29) | collective-permute-done | bytes 1048608 | tf_op jit(solution)/shard_map/ppermute | solution.py:24
  585.3 7.6 collective-permute-done.18
  592.9 11.2 %collective-permute-done.5 = f32[8,8192]{1,0:T(8,128)S(1)} collective-permute-done((f32[8,8192]{1,0:T(8,128)S(1)}, f32[8,8192]{1,0:T(8,128)S(1)}, u32[]{:S(2)}, u32[]{:S(2)}) %collective-permute-start.5) | collective-permute-done | bytes 262176 | tf_op jit(solution)/shard_map/ppermute | solution.py:24
  606.1 6.3 collective-permute-done.6
  629.2 244.3 %psum.14 = f32[14,2,128]{2,1,0:T(2,128)S(1)} all-reduce(f32[14,2,128]{2,1,0:T(2,128)S(1)} %select_add_fusion.9), channel_id=1, replica_groups=mesh['rows'=64,'feat'=4] {'rows'}, use_global_device_ids=true, to_apply=%region_45.50 | all-reduce | flops 3584 | bytes 28672 | tf_op jit(solution)/shard_map/psum | solution.py:180
  873.5 13.4 %psum.15 = f32[14,2,128]{2,1,0:T(2,128)S(1)} all-reduce(f32[14,2,128]{2,1,0:T(2,128)S(1)} %psum.14), channel_id=1, replica_groups=mesh['rows'=64,'feat'=4] {'feat'}, use_global_device_ids=true, to_apply=%region_46.51 | all-reduce | flops 3584 | bytes 28672 | tf_op jit(solution)/shard_map/psum | solution.py:180
  (597 shorter events, 420.1 us)
Async XLA Ops:
  2.1 18.7 %collective-permute-start = (bf16[1024]{0:T(1024)(128)(2,1)S(1)}, bf16[1024]{0:T(1024)(128)(2,1)S(1)}, u32[]{:S(2)}, u32[]{:S(2)}) collective-permute-start(bf16[1024]{0:T(1024)(128)(2,1)S(1)} %and_select_fusion.2), channel_id=1, source_target_pairs={{0,128},{128,0},{4,132},{132,4},{8,136},{136,8},{12,140},{140,12},... | collective-permute-start | bytes 6152 | tf_op jit(solution)/shard_map/ppermute | solution.py:24
  6.6 97.8 %collective-permute-start.13 = (s32[3,1024]{1,0:T(4,128)S(1)}, s32[3,1024]{1,0:T(4,128)S(1)}, u32[]{:S(2)}, u32[]{:S(2)}) collective-permute-start(s32[3,1024]{1,0:T(4,128)S(1)} %concatenate.74), channel_id=1, source_target_pairs={{0,128},{128,0},{4,132},{132,4},{8,136},{136,8},{12,140},{140,12},... | collective-permute-start | bytes 36872 | tf_op jit(solution)/shard_map/ppermute | solution.py:24
  7.4 285.6 %collective-permute-start.1 = (s32[32,1024]{1,0:T(8,128)S(1)}, s32[32,1024]{1,0:T(8,128)S(1)}, u32[]{:S(2)}, u32[]{:S(2)}) collective-permute-start(s32[32,1024]{1,0:T(8,128)S(1)} %concatenate.78), channel_id=1, source_target_pairs={{0,128},{128,0},{4,132},{132,4},{8,136},{136,8},{12,140},{140,12},... | collective-permute-start | bytes 393224 | tf_op jit(solution)/shard_map/ppermute | solution.py:24
  12.1 306.9 %collective-permute-start.2 = (bf16[1024,128]{1,0:T(8,128)(2,1)}, bf16[1024,128]{1,0:T(8,128)(2,1)}, u32[]{:S(2)}, u32[]{:S(2)}) collective-permute-start(bf16[1024,128]{1,0:T(8,128)(2,1)} %concatenate.80), channel_id=1, source_target_pairs={{0,128},{128,0},{4,132},{132,4},{8,136},{136,8},{12,140},{140,12},... | collective-permute-start | bytes 786440 | tf_op jit(solution)/shard_map/ppermute | solution.py:24
  111.1 84.0 %collective-permute-start.25 = (s32[3,1024]{0,1:T(8,128)S(1)}, s32[3,1024]{0,1:T(8,128)S(1)}, u32[]{:S(2)}, u32[]{:S(2)}) collective-permute-start(s32[3,1024]{0,1:T(8,128)S(1)} %bitcast_select_fusion.2), channel_id=1, source_target_pairs={{0,64},{64,0},{4,68},{68,4},{8,72},{72,8},{12,76},{76,12},{16,80},... | collective-permute-start | bytes 36872 | tf_op jit(solution)/shard_map/ppermute | solution.py:24
  199.6 10.6 %collective-permute-start.26 = (bf16[1024]{0:T(1024)(128)(2,1)S(1)}, bf16[1024]{0:T(1024)(128)(2,1)S(1)}, u32[]{:S(2)}, u32[]{:S(2)}) collective-permute-start(bf16[1024]{0:T(1024)(128)(2,1)S(1)} %and_select_fusion), channel_id=1, source_target_pairs={{0,32},{32,0},{4,36},{36,4},{8,40},{40,8},{12,44},{44,12},{16,48},... | collective-permute-start | bytes 6152 | tf_op jit(solution)/shard_map/ppermute | solution.py:24
  298.8 10.4 %collective-permute-start.15 = (s32[32,1024]{0,1:T(8,128)S(1)}, s32[32,1024]{0,1:T(8,128)}, u32[]{:S(2)}, u32[]{:S(2)}) collective-permute-start(s32[32,1024]{0,1:T(8,128)S(1)} %bitcast_select_fusion.3), channel_id=1, source_target_pairs={{0,64},{64,0},{4,68},{68,4},{8,72},{72,8},{12,76},{76,12},{16,80},... | collective-permute-start | bytes 393224 | tf_op jit(solution)/shard_map/ppermute | solution.py:24
  315.7 20.2 %collective-permute-start.27 = (s32[32,1024]{0,1:T(8,128)S(1)}, s32[32,1024]{0,1:T(8,128)}, u32[]{:S(2)}, u32[]{:S(2)}) collective-permute-start(s32[32,1024]{0,1:T(8,128)S(1)} %bitcast_select_fusion.1), channel_id=1, source_target_pairs={{0,32},{32,0},{4,36},{36,4},{8,40},{40,8},{12,44},{44,12},{16,48},... | collective-permute-start | bytes 393224 | tf_op jit(solution)/shard_map/ppermute | solution.py:24
  371.3 9.9 %collective-permute-start.10 = (f32[8,64]{1,0:T(8,128)S(1)}, f32[8,64]{1,0:T(8,128)S(1)}, u32[]{:S(2)}, u32[]{:S(2)}) collective-permute-start(f32[8,64]{1,0:T(8,128)S(1)} %slice_select_fusion.26), channel_id=1, source_target_pairs={{0,16},{16,0},{4,20},{20,4},{8,24},{24,8},{12,28},{28,12},{32,48},... | collective-permute-start | bytes 6152 | tf_op jit(solution)/shard_map/ppermute | solution.py:24
  379.9 10.8 %collective-permute-start.16 = (bf16[1024,128]{1,0:T(8,128)(2,1)S(1)}, bf16[1024,128]{1,0:T(8,128)(2,1)}, u32[]{:S(2)}, u32[]{:S(2)}) collective-permute-start(bf16[1024,128]{1,0:T(8,128)(2,1)S(1)} %get-tuple-element.1187), channel_id=1, source_target_pairs={{0,64},{64,0},{4,68},{68,4},{8,72},{72,8},{12,76},{76,12},{16,80},... | collective-permute-start | bytes 786440 | tf_op jit(solution)/shard_map/ppermute | solution.py:24
  381.2 9.5 %collective-permute-start.11 = (f32[4,64]{1,0:T(4,128)S(1)}, f32[4,64]{1,0:T(4,128)S(1)}, u32[]{:S(2)}, u32[]{:S(2)}) collective-permute-start(f32[4,64]{1,0:T(4,128)S(1)} %slice_select_fusion.28), channel_id=1, source_target_pairs={{0,8},{8,0},{4,12},{12,4},{16,24},{24,16},{20,28},{28,20},{32,40},... | collective-permute-start | bytes 3080 | tf_op jit(solution)/shard_map/ppermute | solution.py:24
  388.2 112.1 %collective-permute-start.3 = (f32[32,8192]{1,0:T(8,128)}, f32[32,8192]{1,0:T(8,128)}, u32[]{:S(2)}, u32[]{:S(2)}) collective-permute-start(f32[32,8192]{1,0:T(8,128)} %select_n.551), channel_id=1, source_target_pairs={{0,64},{64,0},{4,68},{68,4},{8,72},{72,8},{12,76},{76,12},{16,80},... | collective-permute-start | bytes 3145736 | tf_op jit(solution)/shard_map/ppermute | solution.py:24
  418.1 8.6 collective-permute-start.21
  427.7 16.2 %collective-permute-start.28 = (bf16[1024,128]{1,0:T(8,128)(2,1)S(1)}, bf16[1024,128]{1,0:T(8,128)(2,1)}, u32[]{:S(2)}, u32[]{:S(2)}) collective-permute-start(bf16[1024,128]{1,0:T(8,128)(2,1)S(1)} %get-tuple-element.1189), channel_id=1, source_target_pairs={{0,32},{32,0},{4,36},{36,4},{8,40},{40,8},{12,44},{44,12},{16,48},... | collective-permute-start | bytes 786440 | tf_op jit(solution)/shard_map/ppermute | solution.py:24
  431.2 12.7 %collective-permute-start.23 = (f32[8,64]{1,0:T(8,128)S(1)}, f32[8,64]{1,0:T(8,128)S(1)}, u32[]{:S(2)}, u32[]{:S(2)}) collective-permute-start(f32[8,64]{1,0:T(8,128)S(1)} %slice_select_fusion.25), channel_id=1, source_target_pairs={{0,8},{8,0},{4,12},{12,4},{16,24},{24,16},{20,28},{28,20},{32,40},... | collective-permute-start | bytes 6152 | tf_op jit(solution)/shard_map/ppermute | solution.py:24
  437.7 67.3 %collective-permute-start.17 = (f32[32,8192]{1,0:T(8,128)}, f32[32,8192]{1,0:T(8,128)}, u32[]{:S(2)}, u32[]{:S(2)}) collective-permute-start(f32[32,8192]{1,0:T(8,128)} %select_n.589), channel_id=1, source_target_pairs={{0,32},{32,0},{4,36},{36,4},{8,40},{40,8},{12,44},{44,12},{16,48},... | collective-permute-start | bytes 3145736 | tf_op jit(solution)/shard_map/ppermute | solution.py:24
  465.7 26.0 %collective-permute-start.32 = (f32[32,64]{1,0:T(8,128)S(1)}, f32[32,64]{1,0:T(8,128)S(1)}, u32[]{:S(2)}, u32[]{:S(2)}) collective-permute-start(f32[32,64]{1,0:T(8,128)S(1)} %select_n.632), channel_id=1, source_target_pairs={{0,16},{16,0},{4,20},{20,4},{8,24},{24,8},{12,28},{28,12},{32,48},... | collective-permute-start | bytes 24584 | tf_op jit(solution)/shard_map/ppermute | solution.py:24
  465.8 26.0 %collective-permute-start.24 = (f32[4,64]{1,0:T(4,128)S(1)}, f32[4,64]{1,0:T(4,128)S(1)}, u32[]{:S(2)}, u32[]{:S(2)}) collective-permute-start(f32[4,64]{1,0:T(4,128)S(1)} %slice_select_fusion.27), channel_id=1, source_target_pairs={{0,4},{4,0},{8,12},{12,8},{16,20},{20,16},{24,28},{28,24},{32,36},... | collective-permute-start | bytes 3080 | tf_op jit(solution)/shard_map/ppermute | solution.py:24
  499.5 82.2 %collective-permute-start.29 = (f32[32,8192]{1,0:T(8,128)}, f32[32,8192]{1,0:T(8,128)}, u32[]{:S(2)}, u32[]{:S(2)}) collective-permute-start(f32[32,8192]{1,0:T(8,128)} %select_n.621), channel_id=1, source_target_pairs={{0,16},{16,0},{4,20},{20,4},{8,24},{24,8},{12,28},{28,12},{32,48},... | collective-permute-start | bytes 3145736 | tf_op jit(solution)/shard_map/ppermute | solution.py:24
  501.8 81.4 %collective-permute-start.4 = (f32[16,8192]{1,0:T(8,128)S(1)}, f32[16,8192]{1,0:T(8,128)S(1)}, u32[]{:S(2)}, u32[]{:S(2)}) collective-permute-start(f32[16,8192]{1,0:T(8,128)S(1)} %slice_select_fusion.9), channel_id=1, source_target_pairs={{0,32},{32,0},{4,36},{36,4},{8,40},{40,8},{12,44},{44,12},{16,48},... | collective-permute-start | bytes 1572872 | tf_op jit(solution)/shard_map/ppermute | solution.py:24
  506.4 86.4 %collective-permute-start.18 = (f32[16,8192]{1,0:T(8,128)S(1)}, f32[16,8192]{1,0:T(8,128)S(1)}, u32[]{:S(2)}, u32[]{:S(2)}) collective-permute-start(f32[16,8192]{1,0:T(8,128)S(1)} %slice_select_fusion.8), channel_id=1, source_target_pairs={{0,16},{16,0},{4,20},{20,4},{8,24},{24,8},{12,28},{28,12},{32,48},... | collective-permute-start | bytes 1572872 | tf_op jit(solution)/shard_map/ppermute | solution.py:24
  583.0 35.7 %collective-permute-start.30 = (f32[16,8192]{1,0:T(8,128)S(1)}, f32[16,8192]{1,0:T(8,128)S(1)}, u32[]{:S(2)}, u32[]{:S(2)}) collective-permute-start(f32[16,8192]{1,0:T(8,128)S(1)} %slice_select_fusion.7), channel_id=1, source_target_pairs={{0,8},{8,0},{4,12},{12,4},{16,24},{24,16},{20,28},{28,20},{32,40},... | collective-permute-start | bytes 1572872 | tf_op jit(solution)/shard_map/ppermute | solution.py:24
  583.3 20.8 %collective-permute-start.5 = (f32[8,8192]{1,0:T(8,128)S(1)}, f32[8,8192]{1,0:T(8,128)S(1)}, u32[]{:S(2)}, u32[]{:S(2)}) collective-permute-start(f32[8,8192]{1,0:T(8,128)S(1)} %slice_select_fusion.12), channel_id=1, source_target_pairs={{0,16},{16,0},{4,20},{20,4},{8,24},{24,8},{12,28},{28,12},{32,48},... | collective-permute-start | bytes 786440 | tf_op jit(solution)/shard_map/ppermute | solution.py:24
  604.6 13.4 %collective-permute-start.19 = (f32[8,8192]{1,0:T(8,128)S(1)}, f32[8,8192]{1,0:T(8,128)S(1)}, u32[]{:S(2)}, u32[]{:S(2)}) collective-permute-start(f32[8,8192]{1,0:T(8,128)S(1)} %slice_select_fusion.11), channel_id=1, source_target_pairs={{0,8},{8,0},{4,12},{12,4},{16,24},{24,16},{20,28},{28,20},{32,40},... | collective-permute-start | bytes 786440 | tf_op jit(solution)/shard_map/ppermute | solution.py:24
  (32 other events, 303.9 us)
